TPU v7x, 32 devices: a whole 2x2x4 slice. The times are simulated.
32 devices in a mesh: wide: 8 (over z, x), narrow: 4 (over y, core).
Axes of the slice: x: 2, y: 2, z: 4, core: 2. Of those that a mesh axis runs over, the one named last changes fastest.
Arguments:
- points: bfloat16 [32768, 256], P('wide'), may hold values from -6 to 6
- q_init: float32 [16, 32768], P(None, 'wide'), may hold values from -80 to 80
- pairs: int32 [2, 2048], P(None, ('wide', 'narrow')), may hold values from 0 to 255, as said below
Outputs:
- basis: float32 [16, 32768], P(None, 'wide')
- coeffs: float32 [3, 2, 16, 16], replicated
Inputs may be any that keep to these rules, and one draw needn't show every extreme that they name: `pairs`: pair number g * 4 * 64 + m * 64 + o * 8 + c (g < 8, m < 4, o < 8, c < 8) has its first block in g * 32 .. (g + 1) * 32 - 1 and its second block in o * 32 .. (o + 1) * 32 - 1; the two ends of a pair differ.
All inputs are finite; a program needn't handle non-finite values.
Results may differ from a plain program's by a relative error of at most 0.0015.
Values may be sent and summed in bfloat16 or wider, within the bound.
A program may use at most 64 MiB of HBM per device.

v0:
```python
import jax
import jax.numpy as jnp
from jax import lax
from jax.sharding import PartitionSpec as P

BS = 128
STEPS = 3
KERNEL_FACTOR = 3.0
EPSILON = 1e-06
HIGH = lax.Precision.HIGHEST
pair_group = 32


def unit_rows(points):
    wide32 = points.astype(jnp.float32)
    scaled = wide32 * lax.rsqrt(jnp.sum(wide32 * wide32, axis=-1, keepdims=True) + EPSILON)
    return scaled.astype(jnp.bfloat16)


def tile_terms(first_pts, second_pts, first_vec, second_vec):
    inner_products = jnp.einsum(
        "paf,pbf->pab", first_pts, second_pts, preferred_element_type=jnp.float32
    )
    kernel_values = jnp.exp(KERNEL_FACTOR * (inner_products - 1.0))
    to_first = jnp.einsum("pab,prb->pra", kernel_values, second_vec, precision=HIGH)
    to_second = jnp.einsum("pab,pra->prb", kernel_values, first_vec, precision=HIGH)
    return (to_first, to_second)


def per_device(points, q_init, pairs):
    wide_count = lax.axis_size("wide")
    wide_pos = lax.axis_index("wide")
    own_blocks = points.shape[0] // BS
    width = points.shape[1]
    vec_rows = q_init.shape[0]
    pair_count = pairs.shape[1]
    capacity = pair_count // wide_count
    total_points = own_blocks * BS * wide_count
    unit = unit_rows(points).reshape(own_blocks, BS, width)
    first_local = pairs[0] - wide_pos * own_blocks
    wanted = pairs[1].reshape(wide_count, capacity)
    local_ids = (
        lax.all_to_all(wanted, "wide", split_axis=0, concat_axis=0, tiled=True)
        - wide_pos * own_blocks
    )
    replies = lax.all_to_all(unit[local_ids], "wide", split_axis=0, concat_axis=0, tiled=True)
    second_pts = replies
    second_pts = second_pts.reshape(pair_count, BS, width)
    targets = jnp.concatenate([first_local, local_ids.reshape(pair_count)], axis=0)
    owners = (jnp.arange(own_blocks, dtype=jnp.int32)[:, None] == targets[None, :]).astype(
        jnp.float32
    )

    def grouped(values):
        return values.reshape((pair_count // pair_group, pair_group) + values.shape[1:])

    def single_group(items):
        first_ids, second_p, first_v, second_v = items
        return tile_terms(unit[first_ids], second_p, first_v, second_v)

    def gram_sums(values):
        return lax.psum(values, "wide")

    gram0 = gram_sums(jnp.dot(q_init, q_init.T, precision=HIGH)) / total_points
    factor0 = jnp.linalg.cholesky(gram0)
    present_portion = lax.linalg.triangular_solve(factor0, q_init, left_side=True, lower=True)
    current = present_portion
    previous = jnp.zeros_like(present_portion)
    last = jnp.zeros((vec_rows, vec_rows), jnp.float32)
    records = []
    for step in range(STEPS):
        rows = current.reshape(vec_rows, own_blocks, BS).transpose(1, 0, 2)
        second_vec = lax.all_to_all(
            rows[local_ids], "wide", split_axis=0, concat_axis=0, tiled=True
        ).reshape(pair_count, vec_rows, BS)
        first_vec = rows[first_local]
        to_first, to_second = lax.map(
            single_group,
            (grouped(first_local), grouped(second_pts), grouped(first_vec), grouped(second_vec)),
        )
        to_first = to_first.reshape(pair_count, vec_rows * BS)
        returned = lax.all_to_all(
            to_second.reshape(wide_count, capacity, vec_rows * BS),
            "wide",
            split_axis=0,
            concat_axis=0,
            tiled=True,
        )
        terms = jnp.concatenate([to_first, returned.reshape(pair_count, vec_rows * BS)], axis=0)
        summed_blocks = jnp.dot(owners, terms, precision=HIGH)
        summed_blocks = lax.psum(summed_blocks, "narrow")
        image = summed_blocks.reshape(-1, vec_rows, BS).transpose(1, 0, 2).reshape(vec_rows, -1)
        residual = image - jnp.dot(last.T, previous, precision=HIGH)
        raw, cross, basis_gram = gram_sums(
            (
                jnp.dot(residual, residual.T, precision=HIGH),
                jnp.dot(present_portion, residual.T, precision=HIGH),
                jnp.dot(present_portion, present_portion.T, precision=HIGH),
            )
        )
        along = cross / total_points
        raw = raw / total_points
        basis_gram = basis_gram / total_points
        remainder = residual - jnp.dot(along.T, present_portion, precision=HIGH)
        squared = jnp.dot(along.T, along, precision=HIGH)
        gram = (
            raw
            - 2.0 * squared
            + jnp.dot(along.T, jnp.dot(basis_gram, along, precision=HIGH), precision=HIGH)
        )
        factor = jnp.linalg.cholesky(gram)
        records.append(jnp.stack([along, factor]))
        previous = present_portion
        last = factor
        present_portion = lax.linalg.triangular_solve(factor, remainder, left_side=True, lower=True)
        current = present_portion
    return (current, jnp.stack(records))


def solution(mesh):
    placed = (P("wide", None), P(None, "wide"), P(None, ("wide", "narrow")))
    return jax.shard_map(
        per_device, mesh=mesh, in_specs=placed, out_specs=(P(None, "wide"), P()), check_vma=False
    )
```

profile of v0, /device:TPU:0, one launch (start us, length us, event | category | flops | bytes accessed | tf_op | source)
XLA Modules:
  0.0 559.8 jit_solution(13503507722654973966)
XLA Ops:
  8.6 7.3 %all-to-all-start = ((s32[8,1,8]{2,1,0:T(1,128)}), s32[8,1,8]{2,1,0:T(1,128)S(1)}, u32[]{:S(2)}, u32[]{:S(2)}) async-start(s32[8,1,8]{2,1,0:T(1,128)} %bitcast.22), calls=%async_computation | async-start | bytes 8192 | tf_op jit(solution)/shard_map/all_to_all | solution.py:43
  16.4 22.1 %psum.91 = f32[16,16]{1,0:T(8,128)S(1)} all-reduce(f32[16,16]{1,0:T(8,128)S(1)} %fusion.187), channel_id=1, replica_groups=mesh['wide'=8,'narrow'=4] {'wide'}, use_global_device_ids=true, to_apply=%region_1.0 | all-reduce | flops 256 | bytes 2048 | tf_op jit(solution)/shard_map/psum | solution.py:62
  55.1 5.6 %all-to-all-done.1 = f32[8,8,16,128]{3,2,1,0:T(8,128)S(1)} async-done(((f32[8,8,16,128]{3,2,1,0:T(8,128)}), f32[8,8,16,128]{3,2,1,0:T(8,128)S(1)}, u32[]{:S(2)}, u32[]{:S(2)}) %all-to-all-start.1) | async-done | bytes 524320 | tf_op jit(solution)/shard_map/all_to_all | solution.py:73
  60.7 4.7 all-to-all-start.2
  67.0 87.2 %all-to-all-done.2 = bf16[8,8,128,256]{3,2,1,0:T(8,128)(2,1)} async-done(((bf16[8,8,128,256]{3,2,1,0:T(8,128)(2,1)}), bf16[8,8,128,256]{3,2,1,0:T(8,128)(2,1)}, u32[]{:S(2)}, u32[]{:S(2)}) %all-to-all-start.2) | async-done | bytes 4194336 | tf_op jit(solution)/shard_map/all_to_all | solution.py:46
  155.9 23.6 %while.42 = (s32[]{:T(128)}, f32[2,32,16,128]{3,2,1,0:T(8,128)}, f32[2,32,16,128]{3,2,1,0:T(8,128)}, f32[2,32,16,128]{3,2,1,0:T(8,128)S(1)}, s32[2,32]{1,0:T(2,1...) while((s32[]{:T(128)}, f32[2,32,16,128]{3,2,1,0:T(8,128)}, ...), condition=%wide.region_5.8_spmd, body=%wide.region_4.7_spmd.sunk | while | flops 471860320 | bytes 17833084 | solution.py:77
  187.2 12.4 %all-to-all-done.3 = f32[8,8,2048]{2,1,0:T(8,128)S(1)} async-done(((f32[8,8,2048]{2,1,0:T(8,128)}), f32[8,8,2048]{2,1,0:T(8,128)S(1)}, u32[]{:S(2)}, u32[]{:S(2)}) %all-to-all-start.3) | async-done | bytes 524320 | tf_op jit(solution)/shard_map/all_to_all | solution.py:82
  202.4 31.1 %all-reduce.7.cloned.1.call-done = f32[16,4096]{1,0:T(8,128)} async-done(((f32[16,4096]{1,0:T(8,128)}), f32[16,4096]{1,0:T(8,128)}) %all-reduce.7.cloned.1.call-update) | async-done | bytes 262160 | tf_op jit(solution)/shard_map/psum | solution.py:91
  235.6 37.1 %all-reduce.2 = (f32[16,16]{1,0:T(8,128)S(1)}, f32[16,16]{1,0:T(8,128)S(1)}, f32[16,16]{1,0:T(8,128)S(1)}) all-reduce(f32[16,16]{1,0:T(8,128)S(1)} %fusion.189, f32[16,16]{1,0:T(8,128)S(1)} %fusion.188, f32[16,16]{1,0:T(8,128)S(1)} %fusion.190), channel_id=1, replica_groups=mesh['wide'=8,'narrow'=4] {'wide'}, use_global_device_ids=true, to_apply=%region_8.11 | all-reduce | flops 768 | bytes 6144 | tf_op jit(solution)/shard_map/psum | solution.py:62
  285.3 8.8 %all-to-all-done.4 = f32[8,8,16,128]{3,2,1,0:T(8,128)} async-done(((f32[8,8,16,128]{3,2,1,0:T(8,128)}), f32[8,8,16,128]{3,2,1,0:T(8,128)}, u32[]{:S(2)}, u32[]{:S(2)}) %all-to-all-start.4) | async-done | bytes 524320 | tf_op jit(solution)/shard_map/all_to_all | solution.py:73
  295.8 25.6 %while.43 = (s32[]{:T(128)}, f32[2,32,16,128]{3,2,1,0:T(8,128)}, f32[2,32,16,128]{3,2,1,0:T(8,128)}, f32[2,32,16,128]{3,2,1,0:T(8,128)}, s32[2,32]{1,0:T(2,128)S...) while((s32[]{:T(128)}, f32[2,32,16,128]{3,2,1,0:T(8,128)}, ...), condition=%wide.region_11.14_spmd, body=%wide.region_10.13_spmd.sunk | while | flops 471860320 | bytes 17833084 | solution.py:77
  300.7 5.1 fusion.273
  313.5 5.1 fusion.273
  329.0 8.2 %all-to-all-done.5 = f32[8,8,2048]{2,1,0:T(8,128)S(1)} async-done(((f32[8,8,2048]{2,1,0:T(8,128)}), f32[8,8,2048]{2,1,0:T(8,128)S(1)}, u32[]{:S(2)}, u32[]{:S(2)}) %all-to-all-start.5) | async-done | bytes 524320 | tf_op jit(solution)/shard_map/all_to_all | solution.py:82
  339.9 30.2 %all-reduce.9.cloned.1.call-done = f32[16,4096]{1,0:T(8,128)} async-done(((f32[16,4096]{1,0:T(8,128)}), f32[16,4096]{1,0:T(8,128)}) %all-reduce.9.cloned.1.call-update) | async-done | bytes 262160 | tf_op jit(solution)/shard_map/psum | solution.py:91
  373.0 37.1 %all-reduce.1 = (f32[16,16]{1,0:T(8,128)S(1)}, f32[16,16]{1,0:T(8,128)S(1)}, f32[16,16]{1,0:T(8,128)S(1)}) all-reduce(f32[16,16]{1,0:T(8,128)S(1)} %fusion.192, f32[16,16]{1,0:T(8,128)S(1)} %fusion.191, f32[16,16]{1,0:T(8,128)S(1)} %fusion.193), channel_id=1, replica_groups=mesh['wide'=8,'narrow'=4] {'wide'}, use_global_device_ids=true, to_apply=%region_14.17 | all-reduce | flops 768 | bytes 6144 | tf_op jit(solution)/shard_map/psum | solution.py:62
  417.0 4.4 all-to-all-start.6
  422.8 8.6 %all-to-all-done.6 = f32[8,8,16,128]{3,2,1,0:T(8,128)} async-done(((f32[8,8,16,128]{3,2,1,0:T(8,128)}), f32[8,8,16,128]{3,2,1,0:T(8,128)}, u32[]{:S(2)}, u32[]{:S(2)}) %all-to-all-start.6) | async-done | bytes 524320 | tf_op jit(solution)/shard_map/all_to_all | solution.py:73
  433.1 25.6 %while.44 = (s32[]{:T(128)}, f32[2,32,16,128]{3,2,1,0:T(8,128)}, f32[2,32,16,128]{3,2,1,0:T(8,128)}, f32[2,32,16,128]{3,2,1,0:T(8,128)}, s32[2,32]{1,0:T(2,128)S...) while((s32[]{:T(128)}, f32[2,32,16,128]{3,2,1,0:T(8,128)}, ...), condition=%wide.region_17.20_spmd, body=%wide.region_16.19_spmd.sunk | while | flops 471860320 | bytes 17833084 | solution.py:77
  438.0 5.1 fusion.281
  450.8 5.1 fusion.281
  466.0 8.5 %all-to-all-done.7 = f32[8,8,2048]{2,1,0:T(8,128)S(1)} async-done(((f32[8,8,2048]{2,1,0:T(8,128)}), f32[8,8,2048]{2,1,0:T(8,128)S(1)}, u32[]{:S(2)}, u32[]{:S(2)}) %all-to-all-start.7) | async-done | bytes 524320 | tf_op jit(solution)/shard_map/all_to_all | solution.py:82
  475.8 30.6 %all-reduce.11.cloned.1.call-done = f32[16,4096]{1,0:T(8,128)} async-done(((f32[16,4096]{1,0:T(8,128)}), f32[16,4096]{1,0:T(8,128)}) %all-reduce.11.cloned.1.call-update) | async-done | bytes 262160 | tf_op jit(solution)/shard_map/psum | solution.py:91
  509.3 37.1 %all-reduce = (f32[16,16]{1,0:T(8,128)S(1)}, f32[16,16]{1,0:T(8,128)S(1)}, f32[16,16]{1,0:T(8,128)S(1)}) all-reduce(f32[16,16]{1,0:T(8,128)S(1)} %fusion.195, f32[16,16]{1,0:T(8,128)S(1)} %fusion.194, f32[16,16]{1,0:T(8,128)S(1)} %fusion.196), channel_id=1, replica_groups=mesh['wide'=8,'narrow'=4] {'wide'}, use_global_device_ids=true, to_apply=%region_20.23 | all-reduce | flops 768 | bytes 6144 | tf_op jit(solution)/shard_map/psum | solution.py:62
  (171 shorter events, 144.3 us)
Async XLA Ops:
  7.2 8.8 %copy-start = (f32[16,4096]{1,0:T(8,128)S(1)}, f32[16,4096]{1,0:T(8,128)}, u32[]{:S(2)}) copy-start(f32[16,4096]{1,0:T(8,128)} %param.13) | copy-start | bytes 786436
  8.6 36.7 %all-to-all-start = ((s32[8,1,8]{2,1,0:T(1,128)}), s32[8,1,8]{2,1,0:T(1,128)S(1)}, u32[]{:S(2)}, u32[]{:S(2)}) async-start(s32[8,1,8]{2,1,0:T(1,128)} %bitcast.22), calls=%async_computation | async-start | bytes 8192 | tf_op jit(solution)/shard_map/all_to_all | solution.py:43
  46.9 13.9 %all-to-all-start.1 = ((f32[8,8,16,128]{3,2,1,0:T(8,128)}), f32[8,8,16,128]{3,2,1,0:T(8,128)S(1)}, u32[]{:S(2)}, u32[]{:S(2)}) async-start(f32[8,8,16,128]{3,2,1,0:T(8,128)} %bitcast.29), calls=%async_computation.1 | async-start | bytes 1048576 | tf_op jit(solution)/shard_map/all_to_all | solution.py:73
  60.7 4.7 copy-start.4
  60.7 93.5 %all-to-all-start.2 = ((bf16[8,8,128,256]{3,2,1,0:T(8,128)(2,1)}), bf16[8,8,128,256]{3,2,1,0:T(8,128)(2,1)}, u32[]{:S(2)}, u32[]{:S(2)}) async-start(bf16[8,8,128,256]{3,2,1,0:T(8,128)(2,1)} %bitcast.312), calls=%async_computation.2 | async-start | bytes 8388608 | tf_op jit(solution)/shard_map/all_to_all | solution.py:46
  160.9 4.1 copy-start.2
  172.7 4.1 copy-start.2
  181.5 18.2 %all-to-all-start.3 = ((f32[8,8,2048]{2,1,0:T(8,128)}), f32[8,8,2048]{2,1,0:T(8,128)S(1)}, u32[]{:S(2)}, u32[]{:S(2)}) async-start(f32[8,8,2048]{2,1,0:T(8,128)} %reshape.254), calls=%async_computation.3 | async-start | bytes 1048576 | tf_op jit(solution)/shard_map/all_to_all | solution.py:82
  185.0 48.6 %all-reduce.7.cloned.1.call-start = ((), (), s32[]{:S(2)}) async-start(), calls=%async_computation.8 | async-start | bytes 524288 | tf_op jit(solution)/shard_map/psum | solution.py:91
  279.7 14.4 %all-to-all-start.4 = ((f32[8,8,16,128]{3,2,1,0:T(8,128)}), f32[8,8,16,128]{3,2,1,0:T(8,128)}, u32[]{:S(2)}, u32[]{:S(2)}) async-start(f32[8,8,16,128]{3,2,1,0:T(8,128)} %bitcast.324), calls=%async_computation.4 | async-start | bytes 1048576 | tf_op jit(solution)/shard_map/all_to_all | solution.py:73
  300.7 5.1 copy-start.3
  313.5 5.1 copy-start.3
  323.2 13.9 %all-to-all-start.5 = ((f32[8,8,2048]{2,1,0:T(8,128)}), f32[8,8,2048]{2,1,0:T(8,128)S(1)}, u32[]{:S(2)}, u32[]{:S(2)}) async-start(f32[8,8,2048]{2,1,0:T(8,128)} %reshape.261), calls=%async_computation.5 | async-start | bytes 1048576 | tf_op jit(solution)/shard_map/all_to_all | solution.py:82
  326.9 43.2 %all-reduce.9.cloned.1.call-start = ((), (), s32[]{:S(2)}) async-start(), calls=%async_computation.9 | async-start | bytes 524288 | tf_op jit(solution)/shard_map/psum | solution.py:91
  417.0 14.4 %all-to-all-start.6 = ((f32[8,8,16,128]{3,2,1,0:T(8,128)}), f32[8,8,16,128]{3,2,1,0:T(8,128)}, u32[]{:S(2)}, u32[]{:S(2)}) async-start(f32[8,8,16,128]{3,2,1,0:T(8,128)} %bitcast.323), calls=%async_computation.6 | async-start | bytes 1048576 | tf_op jit(solution)/shard_map/all_to_all | solution.py:73
  438.0 5.1 copy-start.1
  450.8 5.1 copy-start.1
  460.6 13.9 %all-to-all-start.7 = ((f32[8,8,2048]{2,1,0:T(8,128)}), f32[8,8,2048]{2,1,0:T(8,128)S(1)}, u32[]{:S(2)}, u32[]{:S(2)}) async-start(f32[8,8,2048]{2,1,0:T(8,128)} %reshape.268), calls=%async_computation.7 | async-start | bytes 1048576 | tf_op jit(solution)/shard_map/all_to_all | solution.py:82
  464.2 42.2 %all-reduce.11.cloned.1.call-start = ((), (), s32[]{:S(2)}) async-start(), calls=%async_computation.10 | async-start | bytes 524288 | tf_op jit(solution)/shard_map/psum | solution.py:91
Sparse Core Ops, SparseCore 0:
  202.1 31.3 all-reduce.6
  339.6 30.4 all-reduce.8
  475.9 30.4 all-reduce.10
where the time goes:
time: 561 us; the launch traced here: 560 us
  waiting for transfers between devices  231 us (41%)
  blocking collectives  133 us (24%)
  matrix products  80.9 us (14%)
  local copies, waits for them, and re-layouts  43.4 us (8%)
  starting transfers between devices  34.9 us (6%)
  other arithmetic  21.7 us (4%)
  between operations  14.1 us (3%)
    psum x4, blocking collectives, gram_sums(): return lax.psum(values, 'wide')  133 us
    psum x3, waiting for transfers between devices, per_device(): summed_blocks = lax.psum(summed_blocks, 'narrow')  91.8 us
    all_to_all x1, waiting for transfers between devices, per_device(): lax.all_to_all(unit[local_ids], 'wide', split_axis=0, concat_axis=0, tile...  87.2 us
    all_to_all x3, waiting for transfers between devices, per_device(): lax.all_to_all(to_second.reshape(wide_count, capacity, vec_rows * BS), 'w...  29.2 us
    dot_general x6, matrix products, tile_terms(): jnp.einsum('pab,prb->pra', kernel_values, second_vec, precision=HIGH)  28.5 us
    all_to_all x3, waiting for transfers between devices, per_device(): lax.all_to_all(rows[local_ids], 'wide', split_axis=0, concat_axis=0, tile...  23.1 us
    dot_general x6, matrix products, tile_terms(): jnp.einsum('paf,pbf->pab', first_pts, second_pts, preferred_element_type=...  17.6 us
    dot_general x6, matrix products, tile_terms(): jnp.einsum('pab,pra->prb', kernel_values, first_vec, precision=HIGH)  16.5 us
  transfers between devices with their start and end apart: 11, of which 10 were waited for; matrix products, arithmetic and copies ran while one was open for 4% of the time, Pallas kernels for 0%

commit v1 on v0

--- a/solution.py
+++ b/solution.py
@@ -9,6 +9,18 @@
 EPSILON = 1e-06
 HIGH = lax.Precision.HIGHEST
 pair_group = 32
+
+
+def split_up(x, dim, peers):
+    dims = x.shape
+    parts = x.reshape(*dims[:dim], peers, dims[dim] // peers, *dims[dim + 1 :])
+    return jnp.moveaxis(parts, dim, 0)
+
+
+def joined_along(blocks, dim):
+    blocks = jnp.moveaxis(blocks, 0, dim)
+    shape = blocks.shape
+    return blocks.reshape(*shape[:dim], shape[dim] * shape[dim + 1], *shape[dim + 2 :])
 
 
 def unit_rows(points):
@@ -79,13 +91,15 @@
             (grouped(first_local), grouped(second_pts), grouped(first_vec), grouped(second_vec)),
         )
         to_first = to_first.reshape(pair_count, vec_rows * BS)
-        returned = lax.all_to_all(
-            to_second.reshape(wide_count, capacity, vec_rows * BS),
-            "wide",
-            split_axis=0,
-            concat_axis=0,
-            tiled=True,
-        )
+        x = to_second.reshape(wide_count, capacity, vec_rows * BS)
+        size, index = (lax.axis_size("wide"), lax.axis_index("wide"))
+        blocks = split_up(x, 0, size)
+        outs = [blocks[index]]
+        for k in range(1, size):
+            sent = blocks[index ^ k]
+            outs.append(lax.ppermute(sent, "wide", [(i, i ^ k) for i in range(size)]))
+        blocks = jnp.stack(outs)[index ^ jnp.arange(size)]
+        returned = joined_along(blocks, 0)
         terms = jnp.concatenate([to_first, returned.reshape(pair_count, vec_rows * BS)], axis=0)
         summed_blocks = jnp.dot(owners, terms, precision=HIGH)
         summed_blocks = lax.psum(summed_blocks, "narrow")

time: 561 us -> 574 us (1.023)
  starting transfers between devices: 34.9 us -> 57.7 us
  waiting for transfers between devices: 231 us -> 209 us
  local copies, waits for them, and re-layouts: 43.4 us -> 55.1 us
    ppermute x0 -> x21, starting transfers between devices: none -> 33.7 us  [per_device(): outs.append(lax.ppermute(sent, 'wide', [(i, i ^ k) for i in range(size)]))]
    all_to_all x3 -> x0, waiting for transfers between devices: 29.2 us -> none  [per_device(): lax.all_to_all(to_second.reshape(wide_count, capacity, vec_rows * BS), 'w...]
    all_to_all x3 -> x0, starting transfers between devices: 10.8 us -> none  [per_device(): lax.all_to_all(to_second.reshape(wide_count, capacity, vec_rows * BS), 'w...]
    ppermute x0 -> x21, waiting for transfers between devices: none -> 7.27 us  [per_device(): outs.append(lax.ppermute(sent, 'wide', [(i, i ^ k) for i in range(size)]))]
    unnamed x10 -> x28, local copies, waits for them, and re-layouts: 5.43 us -> 11.4 us
    reshape x3 -> x0, local copies, waits for them, and re-layouts: 5.75 us -> none  [per_device(): to_second.reshape(wide_count, capacity, vec_rows * BS)]
  transfers between devices with their start and end apart: 11 -> 29, of which waited for: 10 -> 11; matrix products, arithmetic and copies ran while one was open for 4% -> 5% of each run, Pallas kernels for 0% -> 0%
where the time goes in v1:
time: 574 us; the launch traced here: 573 us
  waiting for transfers between devices  209 us (36%)
  blocking collectives  133 us (23%)
  matrix products  81.1 us (14%)
  starting transfers between devices  57.7 us (10%)
  local copies, waits for them, and re-layouts  55.1 us (10%)
  other arithmetic  21.9 us (4%)
  between operations  14.3 us (2%)
    psum x4, blocking collectives, gram_sums(): return lax.psum(values, 'wide')  133 us
    psum x3, waiting for transfers between devices, per_device(): summed_blocks = lax.psum(summed_blocks, 'narrow')  91.8 us
    all_to_all x1, waiting for transfers between devices, per_device(): lax.all_to_all(unit[local_ids], 'wide', split_axis=0, concat_axis=0, tile...  87.1 us
    ppermute x21, starting transfers between devices, per_device(): outs.append(lax.ppermute(sent, 'wide', [(i, i ^ k) for i in range(size)]))  33.7 us
    dot_general x6, matrix products, tile_terms(): jnp.einsum('pab,prb->pra', kernel_values, second_vec, precision=HIGH)  28.5 us
    all_to_all x3, waiting for transfers between devices, per_device(): lax.all_to_all(rows[local_ids], 'wide', split_axis=0, concat_axis=0, tile...  23 us
    dot_general x6, matrix products, tile_terms(): jnp.einsum('paf,pbf->pab', first_pts, second_pts, preferred_element_type=...  17.6 us
    dot_general x6, matrix products, tile_terms(): jnp.einsum('pab,pra->prb', kernel_values, first_vec, precision=HIGH)  16.5 us
  transfers between devices with their start and end apart: 29, of which 11 were waited for; matrix products, arithmetic and copies ran while one was open for 5% of the time, Pallas kernels for 0%

profile of v1, /device:TPU:0, one launch (start us, length us, event | category | flops | bytes accessed | tf_op | source)
XLA Modules:
  0.0 572.7 jit_solution(17660439252031359821)
XLA Ops:
  8.7 7.3 %all-to-all-start = ((s32[8,1,8]{2,1,0:T(1,128)}), s32[8,1,8]{2,1,0:T(1,128)S(1)}, u32[]{:S(2)}, u32[]{:S(2)}) async-start(s32[8,1,8]{2,1,0:T(1,128)} %bitcast.22), calls=%async_computation | async-start | bytes 8192 | tf_op jit(solution)/shard_map/all_to_all | solution.py:55
  16.4 22.1 %psum.91 = f32[16,16]{1,0:T(8,128)S(1)} all-reduce(f32[16,16]{1,0:T(8,128)S(1)} %fusion.188), channel_id=1, replica_groups=mesh['wide'=8,'narrow'=4] {'wide'}, use_global_device_ids=true, to_apply=%region_1.0 | all-reduce | flops 256 | bytes 2048 | tf_op jit(solution)/shard_map/psum | solution.py:74
  55.2 5.6 all-to-all-done.1
  60.8 4.5 all-to-all-start.2
  67.1 87.1 %all-to-all-done.2 = bf16[8,8,128,256]{3,2,1,0:T(8,128)(2,1)} async-done(((bf16[8,8,128,256]{3,2,1,0:T(8,128)(2,1)}), bf16[8,8,128,256]{3,2,1,0:T(8,128)(2,1)}, u32[]{:S(2)}, u32[]{:S(2)}) %all-to-all-start.2) | async-done | bytes 4194336 | tf_op jit(solution)/shard_map/all_to_all | solution.py:58
  155.9 23.6 %while.42 = (s32[]{:T(128)}, f32[2,32,16,128]{3,2,1,0:T(8,128)}, f32[2,32,16,128]{3,2,1,0:T(8,128)}, f32[2,32,16,128]{3,2,1,0:T(8,128)S(1)}, s32[2,32]{1,0:T(2,1...) while((s32[]{:T(128)}, f32[2,32,16,128]{3,2,1,0:T(8,128)}, ...), condition=%wide.region_5.8_spmd, body=%wide.region_4.7_spmd.sunk | while | flops 471860320 | bytes 17833084 | solution.py:89
  160.8 4.1 fusion.266
  172.6 4.1 fusion.266
  204.6 31.2 %all-reduce.7.cloned.1.call-done = f32[16,4096]{1,0:T(8,128)} async-done(((f32[16,4096]{1,0:T(8,128)}), f32[16,4096]{1,0:T(8,128)}) %all-reduce.7.cloned.1.call-update) | async-done | bytes 262160 | tf_op jit(solution)/shard_map/psum | solution.py:105
  237.9 37.1 %all-reduce.2 = (f32[16,16]{1,0:T(8,128)S(1)}, f32[16,16]{1,0:T(8,128)S(1)}, f32[16,16]{1,0:T(8,128)S(1)}) all-reduce(f32[16,16]{1,0:T(8,128)S(1)} %fusion.190, f32[16,16]{1,0:T(8,128)S(1)} %fusion.189, f32[16,16]{1,0:T(8,128)S(1)} %fusion.191), channel_id=1, replica_groups=mesh['wide'=8,'narrow'=4] {'wide'}, use_global_device_ids=true, to_apply=%region_8.11 | all-reduce | flops 768 | bytes 6144 | tf_op jit(solution)/shard_map/psum | solution.py:74
  282.1 4.1 all-to-all-start.3
  287.7 8.8 %all-to-all-done.3 = f32[8,8,16,128]{3,2,1,0:T(8,128)} async-done(((f32[8,8,16,128]{3,2,1,0:T(8,128)}), f32[8,8,16,128]{3,2,1,0:T(8,128)}, u32[]{:S(2)}, u32[]{:S(2)}) %all-to-all-start.3) | async-done | bytes 524320 | tf_op jit(solution)/shard_map/all_to_all | solution.py:85
  298.2 25.6 %while.43 = (s32[]{:T(128)}, f32[2,32,16,128]{3,2,1,0:T(8,128)}, f32[2,32,16,128]{3,2,1,0:T(8,128)}, f32[2,32,16,128]{3,2,1,0:T(8,128)}, s32[2,32]{1,0:T(2,128)S...) while((s32[]{:T(128)}, f32[2,32,16,128]{3,2,1,0:T(8,128)}, ...), condition=%wide.region_11.14_spmd, body=%wide.region_10.13_spmd.sunk | while | flops 471860320 | bytes 17833084 | solution.py:89
  303.2 5.1 fusion.274
  315.9 5.1 fusion.274
  349.1 30.1 %all-reduce.9.cloned.1.call-done = f32[16,4096]{1,0:T(8,128)} async-done(((f32[16,4096]{1,0:T(8,128)}), f32[16,4096]{1,0:T(8,128)}) %all-reduce.9.cloned.1.call-update) | async-done | bytes 262160 | tf_op jit(solution)/shard_map/psum | solution.py:105
  382.1 37.1 %all-reduce.1 = (f32[16,16]{1,0:T(8,128)S(1)}, f32[16,16]{1,0:T(8,128)S(1)}, f32[16,16]{1,0:T(8,128)S(1)}) all-reduce(f32[16,16]{1,0:T(8,128)S(1)} %fusion.193, f32[16,16]{1,0:T(8,128)S(1)} %fusion.192, f32[16,16]{1,0:T(8,128)S(1)} %fusion.194), channel_id=1, replica_groups=mesh['wide'=8,'narrow'=4] {'wide'}, use_global_device_ids=true, to_apply=%region_14.17 | all-reduce | flops 768 | bytes 6144 | tf_op jit(solution)/shard_map/psum | solution.py:74
  426.3 4.1 all-to-all-start.4
  432.2 8.5 %all-to-all-done.4 = f32[8,8,16,128]{3,2,1,0:T(8,128)} async-done(((f32[8,8,16,128]{3,2,1,0:T(8,128)}), f32[8,8,16,128]{3,2,1,0:T(8,128)}, u32[]{:S(2)}, u32[]{:S(2)}) %all-to-all-start.4) | async-done | bytes 524320 | tf_op jit(solution)/shard_map/all_to_all | solution.py:85
  442.4 25.6 %while.44 = (s32[]{:T(128)}, f32[2,32,16,128]{3,2,1,0:T(8,128)}, f32[2,32,16,128]{3,2,1,0:T(8,128)}, f32[2,32,16,128]{3,2,1,0:T(8,128)}, s32[2,32]{1,0:T(2,128)S...) while((s32[]{:T(128)}, f32[2,32,16,128]{3,2,1,0:T(8,128)}, ...), condition=%wide.region_17.20_spmd, body=%wide.region_16.19_spmd.sunk | while | flops 471860320 | bytes 17833084 | solution.py:89
  447.3 5.1 fusion.282
  460.1 5.1 fusion.282
  488.7 30.5 %all-reduce.11.cloned.1.call-done = f32[16,4096]{1,0:T(8,128)} async-done(((f32[16,4096]{1,0:T(8,128)}), f32[16,4096]{1,0:T(8,128)}) %all-reduce.11.cloned.1.call-update) | async-done | bytes 262160 | tf_op jit(solution)/shard_map/psum | solution.py:105
  522.2 37.1 %all-reduce = (f32[16,16]{1,0:T(8,128)S(1)}, f32[16,16]{1,0:T(8,128)S(1)}, f32[16,16]{1,0:T(8,128)S(1)}) all-reduce(f32[16,16]{1,0:T(8,128)S(1)} %fusion.196, f32[16,16]{1,0:T(8,128)S(1)} %fusion.195, f32[16,16]{1,0:T(8,128)S(1)} %fusion.197), channel_id=1, replica_groups=mesh['wide'=8,'narrow'=4] {'wide'}, use_global_device_ids=true, to_apply=%region_20.23 | all-reduce | flops 768 | bytes 6144 | tf_op jit(solution)/shard_map/psum | solution.py:74
  (237 shorter events, 174.5 us)
Async XLA Ops:
  8.7 36.7 %all-to-all-start = ((s32[8,1,8]{2,1,0:T(1,128)}), s32[8,1,8]{2,1,0:T(1,128)S(1)}, u32[]{:S(2)}, u32[]{:S(2)}) async-start(s32[8,1,8]{2,1,0:T(1,128)} %bitcast.22), calls=%async_computation | async-start | bytes 8192 | tf_op jit(solution)/shard_map/all_to_all | solution.py:55
  46.9 13.9 %all-to-all-start.1 = ((f32[8,8,16,128]{3,2,1,0:T(8,128)}), f32[8,8,16,128]{3,2,1,0:T(8,128)S(1)}, u32[]{:S(2)}, u32[]{:S(2)}) async-start(f32[8,8,16,128]{3,2,1,0:T(8,128)} %bitcast.29), calls=%async_computation.1 | async-start | bytes 1048576 | tf_op jit(solution)/shard_map/all_to_all | solution.py:85
  60.8 93.4 %all-to-all-start.2 = ((bf16[8,8,128,256]{3,2,1,0:T(8,128)(2,1)}), bf16[8,8,128,256]{3,2,1,0:T(8,128)(2,1)}, u32[]{:S(2)}, u32[]{:S(2)}) async-start(bf16[8,8,128,256]{3,2,1,0:T(8,128)(2,1)} %bitcast.401), calls=%async_computation.2 | async-start | bytes 8388608 | tf_op jit(solution)/shard_map/all_to_all | solution.py:58
  65.4 170.5 %all-reduce.7.cloned.1.call-start = ((), (), s32[]{:S(2)}) async-start(), calls=%async_computation.5 | async-start | bytes 524288 | tf_op jit(solution)/shard_map/psum | solution.py:105
  181.3 8.4 %collective-permute-start = (f32[1,8,2048]{2,1,0:T(8,128)S(1)}, f32[1,8,2048]{2,1,0:T(8,128)S(1)}, u32[]{:S(2)}, u32[]{:S(2)}) collective-permute-start(f32[1,8,2048]{2,1,0:T(8,128)S(1)} %get-tuple-element.399), channel_id=1, source_target_pairs={{0,4},{4,0},{8,12},{12,8},{16,20},{20,16},{24,28},{28,24},{1,5},{5... | collective-permute-start | bytes 196616 | tf_op jit(solution)/shard_map/ppermute | solution.py:100
  182.6 9.2 %collective-permute-start.1 = (f32[1,8,2048]{2,1,0:T(8,128)S(1)}, f32[1,8,2048]{2,1,0:T(8,128)S(1)}, u32[]{:S(2)}, u32[]{:S(2)}) collective-permute-start(f32[1,8,2048]{2,1,0:T(8,128)S(1)} %get-tuple-element.398), channel_id=1, source_target_pairs={{0,8},{4,12},{8,0},{12,4},{16,24},{20,28},{24,16},{28,20},{1,9},{5... | collective-permute-start | bytes 196616 | tf_op jit(solution)/shard_map/ppermute | solution.py:100
  182.6 12.4 %collective-permute-start.2 = (f32[1,8,2048]{2,1,0:T(8,128)S(1)}, f32[1,8,2048]{2,1,0:T(8,128)S(1)}, u32[]{:S(2)}, u32[]{:S(2)}) collective-permute-start(f32[1,8,2048]{2,1,0:T(8,128)S(1)} %get-tuple-element.397), channel_id=1, source_target_pairs={{0,12},{4,8},{8,4},{12,0},{16,28},{20,24},{24,20},{28,16},{1,13},{... | collective-permute-start | bytes 196616 | tf_op jit(solution)/shard_map/ppermute | solution.py:100
  184.8 10.8 %collective-permute-start.3 = (f32[1,8,2048]{2,1,0:T(8,128)S(1)}, f32[1,8,2048]{2,1,0:T(8,128)S(1)}, u32[]{:S(2)}, u32[]{:S(2)}) collective-permute-start(f32[1,8,2048]{2,1,0:T(8,128)S(1)} %get-tuple-element.396), channel_id=1, source_target_pairs={{0,16},{4,20},{8,24},{12,28},{16,0},{20,4},{24,8},{28,12},{1,17},{... | collective-permute-start | bytes 196616 | tf_op jit(solution)/shard_map/ppermute | solution.py:100
  184.8 11.5 %collective-permute-start.4 = (f32[1,8,2048]{2,1,0:T(8,128)S(1)}, f32[1,8,2048]{2,1,0:T(8,128)S(1)}, u32[]{:S(2)}, u32[]{:S(2)}) collective-permute-start(f32[1,8,2048]{2,1,0:T(8,128)S(1)} %get-tuple-element.395), channel_id=1, source_target_pairs={{0,20},{4,16},{8,28},{12,24},{16,4},{20,0},{24,12},{28,8},{1,21},{... | collective-permute-start | bytes 196616 | tf_op jit(solution)/shard_map/ppermute | solution.py:100
  189.7 7.2 %collective-permute-start.5 = (f32[1,8,2048]{2,1,0:T(8,128)S(1)}, f32[1,8,2048]{2,1,0:T(8,128)S(1)}, u32[]{:S(2)}, u32[]{:S(2)}) collective-permute-start(f32[1,8,2048]{2,1,0:T(8,128)S(1)} %get-tuple-element.394), channel_id=1, source_target_pairs={{0,24},{4,28},{8,16},{12,20},{16,8},{20,12},{24,0},{28,4},{1,25},{... | collective-permute-start | bytes 196616 | tf_op jit(solution)/shard_map/ppermute | solution.py:100
  282.1 14.4 %all-to-all-start.3 = ((f32[8,8,16,128]{3,2,1,0:T(8,128)}), f32[8,8,16,128]{3,2,1,0:T(8,128)}, u32[]{:S(2)}, u32[]{:S(2)}) async-start(f32[8,8,16,128]{3,2,1,0:T(8,128)} %bitcast.413), calls=%async_computation.3 | async-start | bytes 1048576 | tf_op jit(solution)/shard_map/all_to_all | solution.py:85
  286.3 93.0 %all-reduce.9.cloned.1.call-start = ((), (), s32[]{:S(2)}) async-start(), calls=%async_computation.6 | async-start | bytes 524288 | tf_op jit(solution)/shard_map/psum | solution.py:105
  325.6 8.5 %collective-permute-start.7 = (f32[1,8,2048]{2,1,0:T(8,128)S(1)}, f32[1,8,2048]{2,1,0:T(8,128)S(1)}, u32[]{:S(2)}, u32[]{:S(2)}) collective-permute-start(f32[1,8,2048]{2,1,0:T(8,128)S(1)} %get-tuple-element.391), channel_id=1, source_target_pairs={{0,4},{4,0},{8,12},{12,8},{16,20},{20,16},{24,28},{28,24},{1,5},{5... | collective-permute-start | bytes 196616 | tf_op jit(solution)/shard_map/ppermute | solution.py:100
  327.1 9.2 %collective-permute-start.8 = (f32[1,8,2048]{2,1,0:T(8,128)S(1)}, f32[1,8,2048]{2,1,0:T(8,128)S(1)}, u32[]{:S(2)}, u32[]{:S(2)}) collective-permute-start(f32[1,8,2048]{2,1,0:T(8,128)S(1)} %get-tuple-element.390), channel_id=1, source_target_pairs={{0,8},{4,12},{8,0},{12,4},{16,24},{20,28},{24,16},{28,20},{1,9},{5... | collective-permute-start | bytes 196616 | tf_op jit(solution)/shard_map/ppermute | solution.py:100
  327.2 12.0 %collective-permute-start.9 = (f32[1,8,2048]{2,1,0:T(8,128)S(1)}, f32[1,8,2048]{2,1,0:T(8,128)S(1)}, u32[]{:S(2)}, u32[]{:S(2)}) collective-permute-start(f32[1,8,2048]{2,1,0:T(8,128)S(1)} %get-tuple-element.389), channel_id=1, source_target_pairs={{0,12},{4,8},{8,4},{12,0},{16,28},{20,24},{24,20},{28,16},{1,13},{... | collective-permute-start | bytes 196616 | tf_op jit(solution)/shard_map/ppermute | solution.py:100
  329.1 10.8 %collective-permute-start.10 = (f32[1,8,2048]{2,1,0:T(8,128)S(1)}, f32[1,8,2048]{2,1,0:T(8,128)S(1)}, u32[]{:S(2)}, u32[]{:S(2)}) collective-permute-start(f32[1,8,2048]{2,1,0:T(8,128)S(1)} %get-tuple-element.388), channel_id=1, source_target_pairs={{0,16},{4,20},{8,24},{12,28},{16,0},{20,4},{24,8},{28,12},{1,17},{... | collective-permute-start | bytes 196616 | tf_op jit(solution)/shard_map/ppermute | solution.py:100
  329.9 10.7 %collective-permute-start.11 = (f32[1,8,2048]{2,1,0:T(8,128)S(1)}, f32[1,8,2048]{2,1,0:T(8,128)S(1)}, u32[]{:S(2)}, u32[]{:S(2)}) collective-permute-start(f32[1,8,2048]{2,1,0:T(8,128)S(1)} %get-tuple-element.387), channel_id=1, source_target_pairs={{0,20},{4,16},{8,28},{12,24},{16,4},{20,0},{24,12},{28,8},{1,21},{... | collective-permute-start | bytes 196616 | tf_op jit(solution)/shard_map/ppermute | solution.py:100
  426.3 14.4 %all-to-all-start.4 = ((f32[8,8,16,128]{3,2,1,0:T(8,128)}), f32[8,8,16,128]{3,2,1,0:T(8,128)}, u32[]{:S(2)}, u32[]{:S(2)}) async-start(f32[8,8,16,128]{3,2,1,0:T(8,128)} %bitcast.412), calls=%async_computation.4 | async-start | bytes 1048576 | tf_op jit(solution)/shard_map/all_to_all | solution.py:85
  430.4 88.8 %all-reduce.11.cloned.1.call-start = ((), (), s32[]{:S(2)}) async-start(), calls=%async_computation.7 | async-start | bytes 524288 | tf_op jit(solution)/shard_map/psum | solution.py:105
  469.2 9.1 %collective-permute-start.14 = (f32[1,8,2048]{2,1,0:T(8,128)S(1)}, f32[1,8,2048]{2,1,0:T(8,128)S(1)}, u32[]{:S(2)}, u32[]{:S(2)}) collective-permute-start(f32[1,8,2048]{2,1,0:T(8,128)S(1)} %get-tuple-element.383), channel_id=1, source_target_pairs={{0,4},{4,0},{8,12},{12,8},{16,20},{20,16},{24,28},{28,24},{1,5},{5... | collective-permute-start | bytes 196616 | tf_op jit(solution)/shard_map/ppermute | solution.py:100
  471.2 8.6 %collective-permute-start.15 = (f32[1,8,2048]{2,1,0:T(8,128)S(1)}, f32[1,8,2048]{2,1,0:T(8,128)S(1)}, u32[]{:S(2)}, u32[]{:S(2)}) collective-permute-start(f32[1,8,2048]{2,1,0:T(8,128)S(1)} %get-tuple-element.382), channel_id=1, source_target_pairs={{0,8},{4,12},{8,0},{12,4},{16,24},{20,28},{24,16},{28,20},{1,9},{5... | collective-permute-start | bytes 196616 | tf_op jit(solution)/shard_map/ppermute | solution.py:100
  471.4 10.9 %collective-permute-start.16 = (f32[1,8,2048]{2,1,0:T(8,128)S(1)}, f32[1,8,2048]{2,1,0:T(8,128)S(1)}, u32[]{:S(2)}, u32[]{:S(2)}) collective-permute-start(f32[1,8,2048]{2,1,0:T(8,128)S(1)} %get-tuple-element.381), channel_id=1, source_target_pairs={{0,12},{4,8},{8,4},{12,0},{16,28},{20,24},{24,20},{28,16},{1,13},{... | collective-permute-start | bytes 196616 | tf_op jit(solution)/shard_map/ppermute | solution.py:100
  473.2 9.0 %collective-permute-start.17 = (f32[1,8,2048]{2,1,0:T(8,128)S(1)}, f32[1,8,2048]{2,1,0:T(8,128)S(1)}, u32[]{:S(2)}, u32[]{:S(2)}) collective-permute-start(f32[1,8,2048]{2,1,0:T(8,128)S(1)} %get-tuple-element.380), channel_id=1, source_target_pairs={{0,16},{4,20},{8,24},{12,28},{16,0},{20,4},{24,8},{28,12},{1,17},{... | collective-permute-start | bytes 196616 | tf_op jit(solution)/shard_map/ppermute | solution.py:100
  474.0 8.3 %collective-permute-start.18 = (f32[1,8,2048]{2,1,0:T(8,128)S(1)}, f32[1,8,2048]{2,1,0:T(8,128)S(1)}, u32[]{:S(2)}, u32[]{:S(2)}) collective-permute-start(f32[1,8,2048]{2,1,0:T(8,128)S(1)} %get-tuple-element.379), channel_id=1, source_target_pairs={{0,20},{4,16},{8,28},{12,24},{16,4},{20,0},{24,12},{28,8},{1,21},{... | collective-permute-start | bytes 196616 | tf_op jit(solution)/shard_map/ppermute | solution.py:100
  (13 other events, 109.7 us)
Sparse Core Ops, SparseCore 0:
  204.3 31.4 all-reduce.6
  348.8 30.3 all-reduce.8
  488.8 30.3 all-reduce.10
